TPU v7x, 32 devices: a whole 2x2x4 slice. The times are simulated.
32 devices in a mesh: hid: 8 (over z, core), wid: 4 (over y, x).
Axes of the slice: x: 2, y: 2, z: 4, core: 2. Of those that a mesh axis runs over, the one named last changes fastest.
Arguments:
- grad_out: bfloat16 [64, 12288], P('hid', 'wid'), may hold values from -3 to 3
- pre_act: bfloat16 [64, 49152], P(None, 'hid'), may hold values from -6 to 6
- weight: bfloat16 [49152, 12288], P('hid', 'wid'), may hold values from -0.02734375 to 0.02734375
Outputs:
- grad_pre: bfloat16 [64, 49152], P('wid', 'hid')
- grad_weight: bfloat16 [49152, 12288], P('hid', 'wid')
All inputs are finite; a program needn't handle non-finite values.
Results may differ from a plain program's by a relative error of at most 0.0051.
Values may be sent and summed in bfloat16 or wider, within the bound.
No kernel may reach another device: no remote copies, remote signals or barrier semaphores. Data moves between devices by JAX's collectives and lax.ppermute only.
A program may use at most 128 MiB of HBM per device.

v0:
```python
import math
import jax
import jax.numpy as jnp
from jax import lax
from jax.sharding import PartitionSpec as P

coef = math.sqrt(2.0 / math.pi)


def gelu_parts(x):
    inner = coef * (x + 0.044715 * x * x * x)
    tangent = jnp.tanh(inner)
    value = 0.5 * x * (1.0 + tangent)
    slope = 0.5 * (1.0 + tangent) + 0.5 * x * (1.0 - tangent * tangent) * coef * (
        1.0 + 3.0 * 0.044715 * x * x
    )
    return (value, slope)


def contract_rows(left, right):
    return lax.dot_general(
        left, right, (((0,), (0,)), ((), ())), preferred_element_type=jnp.float32
    )


def contract_cols(left, right):
    return lax.dot_general(
        left, right, (((1,), (1,)), ((), ())), preferred_element_type=jnp.float32
    )


def local(grad_out, pre_act, weight):
    value, unused = gelu_parts(pre_act.astype(jnp.float32))
    hidden = value.astype(jnp.bfloat16)
    gathered = lax.all_gather(grad_out, "hid", axis=0, tiled=True)
    grad_w = contract_rows(hidden, gathered)
    partial_value = contract_cols(gathered, weight)
    share = lax.psum_scatter(partial_value, "wid", scatter_dimension=0, tiled=True)
    own_rows = share.shape[0]
    offset = lax.axis_index("wid") * own_rows
    local_pre = lax.dynamic_slice_in_dim(pre_act, offset, own_rows, 0)
    unused_value, slope = gelu_parts(local_pre.astype(jnp.float32))
    grad_pre = (share * slope).astype(jnp.bfloat16)
    return (grad_pre, grad_w.astype(jnp.bfloat16))


def solution(mesh):
    return jax.shard_map(
        local,
        mesh=mesh,
        in_specs=(P("hid", "wid"), P(None, "hid"), P("hid", "wid")),
        out_specs=(P("wid", "hid"), P("hid", "wid")),
        check_vma=False,
    )
```

profile of v0, /device:TPU:0, one launch (start us, length us, event | category | flops | bytes accessed | tf_op | source)
XLA Modules:
  0.0 83.0 jit_solution(14676352917141983411)
XLA Ops:
  7.2 0.0 reduce-scatter.2.cloned.1.call-start
  7.2 16.4 %all_gather.3 = bf16[64,3072]{1,0:T(8,128)(2,1)S(1)} all-gather(bf16[8,3072]{1,0:T(8,128)(2,1)} %param.3), channel_id=1, replica_groups=mesh['hid'=8,'wid'=4] {'hid'}, dimensions={0}, use_global_device_ids=true | all-gather | bytes 442368 | tf_op jit(solution)/shard_map/all_gather | solution.py:35
  23.7 18.2 %fusion.23 = f32[64,6144]{1,0:T(8,128)} fusion(bf16[64,3072]{1,0:T(8,128)(2,1)S(1)} %all_gather.3, bf16[6144,3072]{1,0:T(8,128)(2,1)} %param.5), kind=kOutput, calls=%fused_computation.35 | convolution fusion | flops 2415919104 | bytes 39714816 | tf_op jit(solution)/shard_map/dot_general | solution.py:27
  41.8 0.0 copy-start
  41.8 0.0 reduce-scatter.2.cloned.1.call-update
  41.9 1.1 %copy-done = bf16[64,6144]{1,0:T(8,128)(2,1)S(1)} copy-done((bf16[64,6144]{1,0:T(8,128)(2,1)S(1)}, bf16[64,6144]{1,0:T(8,128)(2,1)}, u32[]{:S(2)}) %copy-start) | copy-done | bytes 786456
  43.0 16.5 %convolution_convert_fusion = bf16[6144,3072]{1,0:T(8,128)(2,1)} fusion(bf16[64,3072]{1,0:T(8,128)(2,1)S(1)} %all_gather.3, bf16[64,6144]{1,0:T(8,128)(2,1)S(1)} %copy-done), kind=kOutput, calls=%fused_computation | convolution fusion | flops 2438725632 | bytes 38928384 | tf_op jit(solution)/shard_map/dot_general | solution.py:21
  59.5 14.7 %reduce-scatter.2.cloned.1.call-done = f32[16,6144]{1,0:T(8,128)} async-done(((f32[64,6144]{1,0:T(8,128)}), f32[16,6144]{1,0:T(8,128)}) %reduce-scatter.2.cloned.1.call-update) | async-done | bytes 393232 | tf_op jit(solution)/shard_map/reduce_scatter | solution.py:38
  74.2 1.9 %fusion.17 = bf16[16,6144]{1,0:T(8,128)(2,1)} fusion(f32[16,6144]{1,0:T(8,128)} %reduce-scatter.2.cloned.1.call-done, bf16[64,6144]{1,0:T(8,128)(2,1)S(1)} %copy-done, s32[]{:T(128)S(6)} %select_n.3), kind=kLoop, calls=%fused_computation.29 | loop fusion | flops 1966080 | bytes 786436 | tf_op jit(solution)/shard_map/convert_element_type | solution.py:43
Async XLA Ops:
  7.2 67.0 %reduce-scatter.2.cloned.1.call-start = ((), (), s32[]{:S(2)}) async-start(), calls=%async_computation.1 | async-start | bytes 1966080 | tf_op jit(solution)/shard_map/reduce_scatter | solution.py:38
  41.8 1.1 %copy-start = (bf16[64,6144]{1,0:T(8,128)(2,1)S(1)}, bf16[64,6144]{1,0:T(8,128)(2,1)}, u32[]{:S(2)}) copy-start(bf16[64,6144]{1,0:T(8,128)(2,1)} %param.4) | copy-start | bytes 2359300
Sparse Core Ops, SparseCore 0:
  42.0 32.1 reduce-scatter.1
where the time goes:
time: 83.2 us; the launch traced here: 83 us
  matrix products  34.7 us (42%)
  blocking collectives  16.4 us (20%)
  waiting for transfers between devices  14.7 us (18%)
  between operations  14 us (17%)
  other arithmetic  1.94 us (2%)
  local copies, waits for them, and re-layouts  1.1 us (1%)
    dot_general x1, matrix products, contract_cols(): lax.dot_general(left, right, (((1,), (1,)), ((), ())), preferred_element_...  18.2 us
    dot_general x1, matrix products, contract_rows(): lax.dot_general(left, right, (((0,), (0,)), ((), ())), preferred_element_...  16.5 us
    all_gather x1, blocking collectives, local(): gathered = lax.all_gather(grad_out, 'hid', axis=0, tiled=True)  16.4 us
    reduce_scatter x1, waiting for transfers between devices, local(): lax.psum_scatter(partial_value, 'wid', scatter_dimension=0, tiled=True)  14.7 us
    convert_element_type x1, other arithmetic, local(): grad_pre = (share * slope).astype(jnp.bfloat16)  1.94 us
  transfers between devices with their start and end apart: 1, of which 1 were waited for; matrix products, arithmetic and copies ran while one was open for 20% of the time, Pallas kernels for 0%

commit v1 on v0

--- a/solution.py
+++ b/solution.py
@@ -32,7 +32,22 @@
 def local(grad_out, pre_act, weight):
     value, unused = gelu_parts(pre_act.astype(jnp.float32))
     hidden = value.astype(jnp.bfloat16)
-    gathered = lax.all_gather(grad_out, "hid", axis=0, tiled=True)
+    ways, here, step = (lax.axis_size("hid"), lax.axis_index("hid"), grad_out.shape[0])
+    dims = [n * ways if d == 0 else n for d, n in enumerate(grad_out.shape)]
+    gathered = lax.dynamic_update_slice_in_dim(
+        jnp.zeros(dims, grad_out.dtype), grad_out, here * step, axis=0
+    )
+    going_up = going_down = grad_out
+    for far in range(1, ways // 2 + 1):
+        going_up = lax.ppermute(going_up, "hid", [(d, (d + 1) % ways) for d in range(ways)])
+        gathered = lax.dynamic_update_slice_in_dim(
+            gathered, going_up, (here - far) % ways * step, axis=0
+        )
+        if 2 * far < ways:
+            going_down = lax.ppermute(going_down, "hid", [(d, (d - 1) % ways) for d in range(ways)])
+            gathered = lax.dynamic_update_slice_in_dim(
+                gathered, going_down, (here + far) % ways * step, axis=0
+            )
     grad_w = contract_rows(hidden, gathered)
     partial_value = contract_cols(gathered, weight)
     share = lax.psum_scatter(partial_value, "wid", scatter_dimension=0, tiled=True)

time: 83.2 us -> 90.1 us (1.083)
  blocking collectives: 16.4 us -> 0 us
  starting transfers between devices: 0.04 us -> 11.7 us
  waiting for transfers between devices: 14.7 us -> 25.4 us
  local copies, waits for them, and re-layouts: 1.1 us -> 2.03 us
    all_gather x1 -> x0, blocking collectives: 16.4 us -> none  [local(): gathered = lax.all_gather(grad_out, 'hid', axis=0, tiled=True)]
    ppermute x0 -> x7, waiting for transfers between devices: none -> 13.5 us  [the longest x4 10.6 us: local(): lax.ppermute(going_up, 'hid', [(d, (d + 1) % ways) for d in range(ways)])]
    ppermute x0 -> x7, starting transfers between devices: none -> 11.6 us  [the longest x3 11.6 us: local(): lax.ppermute(going_down, 'hid', [(d, (d - 1) % ways) for d in range(ways)])]
    reduce_scatter x1, waiting for transfers between devices: 14.7 us -> 11.9 us  [local(): lax.psum_scatter(partial_value, 'wid', scatter_dimension=0, tiled=True)]
  transfers between devices with their start and end apart: 1 -> 8, of which waited for: 1 -> 5; matrix products, arithmetic and copies ran while one was open for 20% -> 19% of each run, Pallas kernels for 0% -> 0%
where the time goes in v1:
time: 90.1 us; the launch traced here: 89.8 us
  matrix products  34.7 us (39%)
  waiting for transfers between devices  25.4 us (28%)
  between operations  14.1 us (16%)
  starting transfers between devices  11.7 us (13%)
  local copies, waits for them, and re-layouts  2.03 us (2%)
  other arithmetic  1.94 us (2%)
    dot_general x1, matrix products, contract_cols(): lax.dot_general(left, right, (((1,), (1,)), ((), ())), preferred_element_...  18.2 us
    dot_general x1, matrix products, contract_rows(): lax.dot_general(left, right, (((0,), (0,)), ((), ())), preferred_element_...  16.5 us
    reduce_scatter x1, waiting for transfers between devices, local(): lax.psum_scatter(partial_value, 'wid', scatter_dimension=0, tiled=True)  11.9 us
    ppermute x3, starting transfers between devices, local(): lax.ppermute(going_down, 'hid', [(d, (d - 1) % ways) for d in range(ways)])  11.6 us
    ppermute x4, waiting for transfers between devices, local(): lax.ppermute(going_up, 'hid', [(d, (d + 1) % ways) for d in range(ways)])  10.6 us
    ppermute x3, waiting for transfers between devices, local(): lax.ppermute(going_down, 'hid', [(d, (d - 1) % ways) for d in range(ways)])  2.86 us
    convert_element_type x1, other arithmetic, local(): grad_pre = (share * slope).astype(jnp.bfloat16)  1.94 us
  transfers between devices with their start and end apart: 8, of which 5 were waited for; matrix products, arithmetic and copies ran while one was open for 19% of the time, Pallas kernels for 0%

profile of v1, /device:TPU:0, one launch (start us, length us, event | category | flops | bytes accessed | tf_op | source)
XLA Modules:
  0.0 89.8 jit_solution(17211316341070625891)
XLA Ops:
  7.2 0.0 reduce-scatter.2.cloned.1.call-start
  7.2 4.6 %collective-permute-start.1 = (bf16[8,3072]{1,0:T(8,128)(2,1)}, bf16[8,3072]{1,0:T(8,128)(2,1)S(1)}, u32[]{:S(2)}, u32[]{:S(2)}) collective-permute-start(bf16[8,3072]{1,0:T(8,128)(2,1)} %param.3), channel_id=1, source_target_pairs={{0,28},{4,0},{8,4},{12,8},{16,12},{20,16},{24,20},{28,24},{1,29},{... | collective-permute-start | bytes 147464 | tf_op jit(solution)/shard_map/ppermute | solution.py:47
  11.8 0.0 collective-permute-start
  11.8 0.8 constant_dynamic-update-slice_fusion.7
  12.7 1.2 %collective-permute-done.1 = bf16[8,3072]{1,0:T(8,128)(2,1)S(1)} collective-permute-done((bf16[8,3072]{1,0:T(8,128)(2,1)}, bf16[8,3072]{1,0:T(8,128)(2,1)S(1)}, u32[]{:S(2)}, u32[]{:S(2)}) %collective-permute-start.1) | collective-permute-done | bytes 49184 | tf_op jit(solution)/shard_map/ppermute | solution.py:47
  13.8 3.5 %collective-permute-start.3 = (bf16[8,3072]{1,0:T(8,128)(2,1)S(1)}, bf16[8,3072]{1,0:T(8,128)(2,1)S(1)}, u32[]{:S(2)}, u32[]{:S(2)}) collective-permute-start(bf16[8,3072]{1,0:T(8,128)(2,1)S(1)} %collective-permute-done.1), channel_id=1, source_target_pairs={{0,28},{4,0},{8,4},{12,8},{16,12},{20,16},{24,20},{28,24},{1,29},{... | collective-permute-start | bytes 147464 | tf_op jit(solution)/shard_map/ppermute | solution.py:47
  17.3 0.0 collective-permute-done
  17.4 0.0 collective-permute-start.2
  17.4 1.7 %collective-permute-done.3 = bf16[8,3072]{1,0:T(8,128)(2,1)S(1)} collective-permute-done((bf16[8,3072]{1,0:T(8,128)(2,1)S(1)}, bf16[8,3072]{1,0:T(8,128)(2,1)S(1)}, u32[]{:S(2)}, u32[]{:S(2)}) %collective-permute-start.3) | collective-permute-done | bytes 49184 | tf_op jit(solution)/shard_map/ppermute | solution.py:47
  19.1 3.6 %collective-permute-start.5 = (bf16[8,3072]{1,0:T(8,128)(2,1)S(1)}, bf16[8,3072]{1,0:T(8,128)(2,1)S(1)}, u32[]{:S(2)}, u32[]{:S(2)}) collective-permute-start(bf16[8,3072]{1,0:T(8,128)(2,1)S(1)} %collective-permute-done.3), channel_id=1, source_target_pairs={{0,28},{4,0},{8,4},{12,8},{16,12},{20,16},{24,20},{28,24},{1,29},{... | collective-permute-start | bytes 147464 | tf_op jit(solution)/shard_map/ppermute | solution.py:47
  22.6 0.0 collective-permute-done.2
  22.7 0.0 collective-permute-start.4
  22.7 5.3 %collective-permute-done.4 = bf16[8,3072]{1,0:T(8,128)(2,1)S(1)} collective-permute-done((bf16[8,3072]{1,0:T(8,128)(2,1)S(1)}, bf16[8,3072]{1,0:T(8,128)(2,1)S(1)}, u32[]{:S(2)}, u32[]{:S(2)}) %collective-permute-start.4) | collective-permute-done | bytes 49184 | tf_op jit(solution)/shard_map/ppermute | solution.py:42
  28.0 0.0 collective-permute-start.6
  28.0 0.0 collective-permute-done.5
  28.0 5.3 %collective-permute-done.6 = bf16[8,3072]{1,0:T(8,128)(2,1)S(1)} collective-permute-done((bf16[8,3072]{1,0:T(8,128)(2,1)S(1)}, bf16[8,3072]{1,0:T(8,128)(2,1)S(1)}, u32[]{:S(2)}, u32[]{:S(2)}) %collective-permute-start.6) | collective-permute-done | bytes 49184 | tf_op jit(solution)/shard_map/ppermute | solution.py:42
  33.3 18.2 %fusion.23 = f32[64,6144]{1,0:T(8,128)} fusion(bf16[64,3072]{1,0:T(8,128)(2,1)S(1)} %constant_dynamic-update-slice_fusion, bf16[6144,3072]{1,0:T(8,128)(2,1)} %param.5), kind=kOutput, calls=%fused_computation.43 | convolution fusion | flops 2415919104 | bytes 39714816 | tf_op jit(solution)/shard_map/dot_general | solution.py:27
  51.5 0.0 copy-start
  51.5 0.0 reduce-scatter.2.cloned.1.call-update
  51.5 1.1 %copy-done = bf16[64,6144]{1,0:T(8,128)(2,1)S(1)} copy-done((bf16[64,6144]{1,0:T(8,128)(2,1)S(1)}, bf16[64,6144]{1,0:T(8,128)(2,1)}, u32[]{:S(2)}) %copy-start) | copy-done | bytes 786456
  52.6 16.5 %convolution_convert_fusion = bf16[6144,3072]{1,0:T(8,128)(2,1)} fusion(bf16[64,3072]{1,0:T(8,128)(2,1)S(1)} %constant_dynamic-update-slice_fusion, bf16[64,6144]{1,0:T(8,128)(2,1)S(1)} %copy-done), kind=kOutput, calls=%fused_computation | convolution fusion | flops 2438725632 | bytes 38928384 | tf_op jit(solution)/shard_map/dot_general | solution.py:21
  69.1 11.9 %reduce-scatter.2.cloned.1.call-done = f32[16,6144]{1,0:T(8,128)} async-done(((f32[64,6144]{1,0:T(8,128)}), f32[16,6144]{1,0:T(8,128)}) %reduce-scatter.2.cloned.1.call-update) | async-done | bytes 393232 | tf_op jit(solution)/shard_map/reduce_scatter | solution.py:53
  81.0 1.9 %fusion.17 = bf16[16,6144]{1,0:T(8,128)(2,1)} fusion(f32[16,6144]{1,0:T(8,128)} %reduce-scatter.2.cloned.1.call-done, bf16[64,6144]{1,0:T(8,128)(2,1)S(1)} %copy-done, s32[]{:T(128)S(6)} %select_n.73), kind=kLoop, calls=%fused_computation.29 | loop fusion | flops 1966080 | bytes 786436 | tf_op jit(solution)/shard_map/convert_element_type | solution.py:58
  (8 shorter events, 0.1 us)
Async XLA Ops:
  7.2 73.8 %reduce-scatter.2.cloned.1.call-start = ((), (), s32[]{:S(2)}) async-start(), calls=%async_computation.1 | async-start | bytes 1966080 | tf_op jit(solution)/shard_map/reduce_scatter | solution.py:53
  7.2 6.6 %collective-permute-start.1 = (bf16[8,3072]{1,0:T(8,128)(2,1)}, bf16[8,3072]{1,0:T(8,128)(2,1)S(1)}, u32[]{:S(2)}, u32[]{:S(2)}) collective-permute-start(bf16[8,3072]{1,0:T(8,128)(2,1)} %param.3), channel_id=1, source_target_pairs={{0,28},{4,0},{8,4},{12,8},{16,12},{20,16},{24,20},{28,24},{1,29},{... | collective-permute-start | bytes 147464 | tf_op jit(solution)/shard_map/ppermute | solution.py:47
  11.8 5.6 %collective-permute-start = (bf16[8,3072]{1,0:T(8,128)(2,1)}, bf16[8,3072]{1,0:T(8,128)(2,1)S(1)}, u32[]{:S(2)}, u32[]{:S(2)}) collective-permute-start(bf16[8,3072]{1,0:T(8,128)(2,1)} %param.3), channel_id=1, source_target_pairs={{0,4},{4,8},{8,12},{12,16},{16,20},{20,24},{24,28},{28,0},{1,5},{5... | collective-permute-start | bytes 147464 | tf_op jit(solution)/shard_map/ppermute | solution.py:42
  13.8 5.2 %collective-permute-start.3 = (bf16[8,3072]{1,0:T(8,128)(2,1)S(1)}, bf16[8,3072]{1,0:T(8,128)(2,1)S(1)}, u32[]{:S(2)}, u32[]{:S(2)}) collective-permute-start(bf16[8,3072]{1,0:T(8,128)(2,1)S(1)} %collective-permute-done.1), channel_id=1, source_target_pairs={{0,28},{4,0},{8,4},{12,8},{16,12},{20,16},{24,20},{28,24},{1,29},{... | collective-permute-start | bytes 147464 | tf_op jit(solution)/shard_map/ppermute | solution.py:47
  17.4 5.3 %collective-permute-start.2 = (bf16[8,3072]{1,0:T(8,128)(2,1)S(1)}, bf16[8,3072]{1,0:T(8,128)(2,1)S(1)}, u32[]{:S(2)}, u32[]{:S(2)}) collective-permute-start(bf16[8,3072]{1,0:T(8,128)(2,1)S(1)} %collective-permute-done), channel_id=1, source_target_pairs={{0,4},{4,8},{8,12},{12,16},{16,20},{20,24},{24,28},{28,0},{1,5},{5... | collective-permute-start | bytes 147464 | tf_op jit(solution)/shard_map/ppermute | solution.py:42
  19.1 8.9 %collective-permute-start.5 = (bf16[8,3072]{1,0:T(8,128)(2,1)S(1)}, bf16[8,3072]{1,0:T(8,128)(2,1)S(1)}, u32[]{:S(2)}, u32[]{:S(2)}) collective-permute-start(bf16[8,3072]{1,0:T(8,128)(2,1)S(1)} %collective-permute-done.3), channel_id=1, source_target_pairs={{0,28},{4,0},{8,4},{12,8},{16,12},{20,16},{24,20},{28,24},{1,29},{... | collective-permute-start | bytes 147464 | tf_op jit(solution)/shard_map/ppermute | solution.py:47
  22.7 5.3 %collective-permute-start.4 = (bf16[8,3072]{1,0:T(8,128)(2,1)S(1)}, bf16[8,3072]{1,0:T(8,128)(2,1)S(1)}, u32[]{:S(2)}, u32[]{:S(2)}) collective-permute-start(bf16[8,3072]{1,0:T(8,128)(2,1)S(1)} %collective-permute-done.2), channel_id=1, source_target_pairs={{0,4},{4,8},{8,12},{12,16},{16,20},{20,24},{24,28},{28,0},{1,5},{5... | collective-permute-start | bytes 147464 | tf_op jit(solution)/shard_map/ppermute | solution.py:42
  28.0 5.3 %collective-permute-start.6 = (bf16[8,3072]{1,0:T(8,128)(2,1)S(1)}, bf16[8,3072]{1,0:T(8,128)(2,1)S(1)}, u32[]{:S(2)}, u32[]{:S(2)}) collective-permute-start(bf16[8,3072]{1,0:T(8,128)(2,1)S(1)} %collective-permute-done.4), channel_id=1, source_target_pairs={{0,4},{4,8},{8,12},{12,16},{16,20},{20,24},{24,28},{28,0},{1,5},{5... | collective-permute-start | bytes 147464 | tf_op jit(solution)/shard_map/ppermute | solution.py:42
  51.5 1.1 %copy-start = (bf16[64,6144]{1,0:T(8,128)(2,1)S(1)}, bf16[64,6144]{1,0:T(8,128)(2,1)}, u32[]{:S(2)}) copy-start(bf16[64,6144]{1,0:T(8,128)(2,1)} %param.4) | copy-start | bytes 2359300
Sparse Core Ops, SparseCore 0:
  51.6 29.3 reduce-scatter.1
